TPU v7x, 256 devices: a whole 4x4x8 slice. The times are simulated.
256 devices in a mesh: dp: 32 (over x, z), expert: 8 (over y, core).
Axes of the slice: x: 4, y: 4, z: 8, core: 2. Of those that a mesh axis runs over, the one named last changes fastest.
Arguments:
- tokens: bfloat16 [32768, 2048], P(('dp', 'expert')), may hold values from -24 to 24
- expert_ids: int32 [32768, 4], P(('dp', 'expert')), may hold values from 0 to 7, all different within a row; in each aligned block of 128 rows (0 to 127, 128 to 255, ...) at most 128 rows name the same one
- gates: bfloat16 [32768, 4], P(('dp', 'expert')), may hold values from 0.099609375 to 1
- w_gate: bfloat16 [8, 2048, 384], P('expert'), may hold values from -0.125 to 0.125
- w_up: bfloat16 [8, 2048, 384], P('expert'), may hold values from -0.125 to 0.125
- w_down: bfloat16 [8, 384, 2048], P('expert'), may hold values from -0.3125 to 0.3125
- cotangent: bfloat16 [32768, 2048], P(('dp', 'expert')), may hold values from -6 to 6
Outputs:
- mixed: bfloat16 [32768, 2048], P(('dp', 'expert'))
- grad_tokens: bfloat16 [32768, 2048], P(('dp', 'expert'))
- grad_gate: float32 [8, 2048, 384], P('expert', 'dp')
- grad_up: float32 [8, 2048, 384], P('expert', 'dp')
- grad_down: float32 [8, 384, 2048], P('expert', 'dp')
Inputs may be any that keep to these rules, and one draw needn't show every extreme that they name: `expert_ids`: each row names 4 different experts. In each aligned block of 128 rows (the rows of one device) no expert is named by more than 128 rows, a bound that some block reaches.
All inputs are finite; a program needn't handle non-finite values.
Results may differ from a plain program's by a relative error of at most 0.024.
Values may be sent and summed in bfloat16 or wider, within the bound.
A program may use at most 128 MiB of HBM per device.

v0:
```python
import jax
import jax.numpy as jnp
from jax import lax
from jax.sharding import PartitionSpec as P


def expert_rows(inputs, out_grads, gate_col, gate_panel, up_panel, down_panel):
    pre_gate = jnp.dot(inputs, gate_panel, preferred_element_type=jnp.float32)
    pre_up = jnp.dot(inputs, up_panel, preferred_element_type=jnp.float32)
    gate_sigmoid = jax.nn.sigmoid(pre_gate)
    activated = (pre_gate * gate_sigmoid * pre_up).astype(jnp.bfloat16)
    expert_out = jnp.dot(activated, down_panel, preferred_element_type=jnp.float32)
    contrib = (gate_col.astype(jnp.float32)[:, None] * expert_out).astype(jnp.bfloat16)
    act_grad = lax.dot_general(
        out_grads, down_panel, (((1,), (1,)), ((), ())), preferred_element_type=jnp.float32
    )
    up_grad = (act_grad * pre_gate * gate_sigmoid).astype(jnp.bfloat16)
    pre_grad = (act_grad * pre_up * gate_sigmoid * (1.0 + pre_gate * (1.0 - gate_sigmoid))).astype(
        jnp.bfloat16
    )
    grad_rows = lax.dot_general(
        pre_grad, gate_panel, (((1,), (1,)), ((), ())), preferred_element_type=jnp.float32
    )
    grad_rows = grad_rows + lax.dot_general(
        up_grad, up_panel, (((1,), (1,)), ((), ())), preferred_element_type=jnp.float32
    )
    grad_rows = grad_rows.astype(jnp.bfloat16)
    wgrad_gate = lax.dot_general(
        inputs, pre_grad, (((0,), (0,)), ((), ())), preferred_element_type=jnp.float32
    )
    wgrad_up = lax.dot_general(
        inputs, up_grad, (((0,), (0,)), ((), ())), preferred_element_type=jnp.float32
    )
    wgrad_down = lax.dot_general(
        activated, out_grads, (((0,), (0,)), ((), ())), preferred_element_type=jnp.float32
    )
    return (contrib, grad_rows, wgrad_gate, wgrad_up, wgrad_down)


def slot_table(route_ids, expert_num, per_source):
    token_count, pick_count = route_ids.shape
    matches = route_ids == expert_num
    hit_rows = jnp.any(matches, axis=1).astype(jnp.int32)
    which_pick = jnp.sum(
        matches.astype(jnp.int32) * jnp.arange(pick_count, dtype=jnp.int32)[None, :], axis=1
    )
    rank_of = jnp.cumsum(hit_rows) - hit_rows
    wanted = jnp.arange(per_source, dtype=jnp.int32)
    chosen = ((hit_rows[None, :] == 1) & (rank_of[None, :] == wanted[:, None])).astype(jnp.int32)
    valid_slot = jnp.sum(chosen, axis=1) > 0
    row_of = jnp.sum(chosen * jnp.arange(token_count, dtype=jnp.int32)[None, :], axis=1)
    pick_of = jnp.sum(chosen * which_pick[None, :], axis=1)
    return (row_of, pick_of, valid_slot)


def per_device(tokens, expert_ids, gates, w_gate, w_up, w_down, cotangent):
    tok_dev, model_width = tokens.shape
    group_size = lax.axis_size("expert")
    slot_count = group_size * tok_dev
    my_expert = lax.axis_index("expert")
    gate_panel = w_gate[0]
    up_panel = w_up[0]
    down_panel = w_down[0]
    all_rows, all_cot, all_gates = (
        lax.all_gather(tokens, "expert", axis=0, tiled=True),
        lax.all_gather(cotangent, "expert", axis=0, tiled=True),
        lax.all_gather(gates, "expert", axis=0, tiled=True),
    )
    all_ids = lax.all_gather(expert_ids, "expert", axis=0, tiled=True)
    source_ids = all_ids.reshape(group_size, tok_dev, all_ids.shape[1])
    row_of, pick_of, keep_mask = jax.vmap(
        lambda route_ids: slot_table(route_ids, my_expert, tok_dev)
    )(source_ids)
    flat_row = (row_of + jnp.arange(group_size, dtype=jnp.int32)[:, None] * tok_dev).reshape(
        slot_count
    )
    keep_b = keep_mask.reshape(slot_count).astype(jnp.bfloat16)
    inputs = all_rows[flat_row] * keep_b[:, None]
    gate_col = all_gates[flat_row, pick_of.reshape(slot_count)] * keep_b
    out_grads = (
        gate_col.astype(jnp.float32)[:, None] * all_cot[flat_row].astype(jnp.float32)
    ).astype(jnp.bfloat16)
    contrib, grad_rows, acc_gate, acc_up, acc_down = expert_rows(
        inputs, out_grads, gate_col, gate_panel, up_panel, down_panel
    )
    dest = jnp.where(keep_mask.reshape(slot_count), flat_row, group_size * tok_dev)
    part_out = (
        jnp.zeros((group_size * tok_dev, model_width), jnp.float32)
        .at[dest]
        .set(contrib.astype(jnp.float32), mode="drop")
    )
    part_grad = (
        jnp.zeros((group_size * tok_dev, model_width), jnp.float32)
        .at[dest]
        .set(grad_rows.astype(jnp.float32), mode="drop")
    )
    summed_out, summed_grad = (
        lax.psum_scatter(
            part_out.astype(jnp.bfloat16), "expert", scatter_dimension=0, tiled=True
        ).astype(jnp.float32),
        lax.psum_scatter(
            part_grad.astype(jnp.bfloat16), "expert", scatter_dimension=0, tiled=True
        ).astype(jnp.float32),
    )
    mixed = summed_out.astype(jnp.bfloat16)
    grad_tokens = summed_grad.astype(jnp.bfloat16)
    grad_gate, grad_up, grad_down = (
        lax.psum_scatter(
            acc_gate.astype(jnp.bfloat16), "dp", scatter_dimension=0, tiled=True
        ).astype(jnp.float32),
        lax.psum_scatter(acc_up.astype(jnp.bfloat16), "dp", scatter_dimension=0, tiled=True).astype(
            jnp.float32
        ),
        lax.psum_scatter(
            acc_down.astype(jnp.bfloat16), "dp", scatter_dimension=0, tiled=True
        ).astype(jnp.float32),
    )
    return (mixed, grad_tokens, grad_gate[None], grad_up[None], grad_down[None])


def solution(mesh):
    return jax.shard_map(
        per_device,
        mesh=mesh,
        in_specs=(
            P(("dp", "expert"), None),
            P(("dp", "expert"), None),
            P(("dp", "expert"), None),
            P("expert", None, None),
            P("expert", None, None),
            P("expert", None, None),
            P(("dp", "expert"), None),
        ),
        out_specs=(
            P(("dp", "expert"), None),
            P(("dp", "expert"), None),
            P("expert", "dp", None),
            P("expert", "dp", None),
            P("expert", "dp", None),
        ),
        check_vma=False,
    )
```

profile of v0, /device:TPU:2, one launch (start us, length us, event | category | flops | bytes accessed | tf_op | source)
XLA Modules:
  0.0 633.2 jit_solution(9545320917792145153)
XLA Ops:
  7.2 0.0 copy-start
  7.2 0.0 all-gather.3.cloned.1.call-start
  7.2 0.7 all-gather.3.cloned.1.call-update
  7.9 0.0 all-gather.5.cloned.1.call-start
  8.0 0.7 all-gather.5.cloned.1.call-update
  8.7 0.0 reduce-scatter.13.cloned.1.call-start
  8.7 12.2 %all_gather.12 = s32[1024,4]{0,1:T(4,128)S(1)} all-gather(s32[128,4]{0,1:T(4,128)} %param.8), channel_id=1, replica_groups=mesh['dp'=32,'expert'=8] {'expert'}, dimensions={0}, use_global_device_ids=true | all-gather | bytes 18432 | tf_op jit(solution)/shard_map/all_gather | solution.py:69
  21.0 0.3 reduce_window_sum.11
  21.3 9.9 %all_gather.13 = bf16[1024,4]{0,1:T(4,128)(2,1)S(1)} all-gather(bf16[128,4]{0,1:T(4,128)(2,1)} %param.9), channel_id=1, replica_groups=mesh['dp'=32,'expert'=8] {'expert'}, dimensions={0}, use_global_device_ids=true | all-gather | bytes 9216 | tf_op jit(solution)/shard_map/all_gather | solution.py:67
  31.2 0.5 select_reduce_fusion
  31.7 0.1 broadcast_add_fusion
  31.8 9.1 %gather_fusion = bf16[1024]{0:T(1024)(128)(2,1)S(1)} fusion(bf16[1024,4]{0,1:T(4,128)(2,1)S(1)} %all_gather.13, s32[1024]{0:T(1024)S(1)} %bitcast.63), kind=kCustom, calls=%fused_computation | custom fusion | bytes 12288 | tf_op jit(solution)/shard_map/gather | solution.py:79
  40.9 6.6 %all-gather.3.cloned.1.call-done = bf16[1024,2048]{1,0:T(8,128)(2,1)} async-done(((bf16[128,2048]{1,0:T(8,128)(2,1)}), bf16[1024,2048]{1,0:T(8,128)(2,1)}) %all-gather.3.cloned.1.call-update) | async-done | bytes 4194320 | tf_op jit(solution)/shard_map/all_gather | solution.py:65
  47.6 11.5 %gather_fusion.1 = bf16[1024,2048]{1,0:T(8,128)(2,1)} fusion(bf16[1024,2048]{1,0:T(8,128)(2,1)} %all-gather.3.cloned.1.call-done, s32[1024]{0:T(1024)S(1)} %broadcast_clamp_fusion), kind=kCustom, calls=%fused_computation.1 | custom fusion | bytes 8392704 | tf_op jit(solution)/shard_map/gather | solution.py:78
  59.1 6.6 %fusion.9 = f32[1024,384]{1,0:T(8,128)} fusion(bf16[1024,2048]{1,0:T(8,128)(2,1)} %gather_fusion.1, bf16[1024]{0:T(1024)(128)(2,1)S(1)} %bitcast_convert_fusion.2, bf16[1,2048,384]{2,1,0:T(8,128)(2,1)} %param.11), kind=kOutput, calls=%fused_computation.19 | convolution fusion | flops 1612709888 | bytes 7342080 | tf_op jit(solution)/shard_map/dot_general | solution.py:9
  65.7 3.6 fusion.11
  69.3 14.8 %all-gather.5.cloned.1.call-done = bf16[1024,2048]{1,0:T(8,128)(2,1)} async-done(((bf16[128,2048]{1,0:T(8,128)(2,1)}), bf16[1024,2048]{1,0:T(8,128)(2,1)}) %all-gather.5.cloned.1.call-update) | async-done | bytes 4194320 | tf_op jit(solution)/shard_map/all_gather | solution.py:66
  84.1 11.5 %gather_fusion.2 = bf16[1024,2048]{1,0:T(8,128)(2,1)} fusion(bf16[1024,2048]{1,0:T(8,128)(2,1)} %all-gather.5.cloned.1.call-done, s32[1024]{0:T(1024)S(1)} %broadcast_clamp_fusion), kind=kCustom, calls=%fused_computation.2 | custom fusion | bytes 8392704 | tf_op jit(solution)/shard_map/gather | solution.py:81
  95.6 7.3 %multiply_convert_fusion.4 = (bf16[1024,384]{1,0:T(8,128)(2,1)S(1)}, bf16[1024,384]{1,0:T(8,128)(2,1)}, bf16[1024,384]{1,0:T(8,128)(2,1)}) fusion(f32[1024,384]{1,0:T(8,128)} %fusion.11, f32[1024,384]{1,0:T(8,128)} %fusion.9, bf16[1,384,2048]{2,1,0:T(8,128)(2,1)S(1)} %copy-done, bf16[1024,2048]{1,0:T(8,128)(2,1)} %gather_fusion.2, ...), kind=kOutput, calls=%fused_computation.35 | convolution fusion | flops 1623195648 | bytes 11276288 | tf_op jit(solution)/shard_map/dot_general | solution.py:14
  103.0 0.9 copy-done.5
  103.9 3.8 convolution_convert_fusion.1
  107.6 0.0 reduce-scatter.13.cloned.1.call-update
  107.7 0.2 reduce-scatter.11.cloned.1.call-start
  107.9 6.1 convolution_convert_fusion.2
  114.0 0.0 reduce-scatter.11.cloned.1.call-update
  114.0 0.0 reduce-scatter.7.cloned.1.call-start
  114.1 5.4 multiply_convert_fusion.1
  119.5 10.9 %scatter_custom_fusion = f32[1024,2048]{1,0:T(8,128)} fusion(s32[1024]{0:T(1024)S(1)} %bitcast.70, bf16[1024,2048]{1,0:T(8,128)(2,1)} %multiply_convert_fusion.1, f32[]{:T(128)} %constant.10.clone.1), kind=kCustom, calls=%fused_computation.9 | custom fusion | flops 2097152 | bytes 12582916 | tf_op jit(solution)/shard_map/scatter | solution.py:90
  130.4 6.0 convert_element_type.93
  136.4 0.0 reduce-scatter.7.cloned.1.call-update
  136.4 0.3 reduce-scatter.9.cloned.1.call-start
  136.7 0.0 copy-start.4
  136.7 3.6 fusion.22
  140.4 4.3 add_convert_fusion
  144.7 11.0 %scatter_custom_fusion.1 = f32[1024,2048]{1,0:T(8,128)} fusion(s32[1024]{0:T(1024)S(1)} %bitcast.71, bf16[1024,2048]{1,0:T(8,128)(2,1)} %add_convert_fusion, f32[]{:T(128)} %constant.10.clone.1), kind=kCustom, calls=%fused_computation.5 | custom fusion | flops 2097152 | bytes 12582916 | tf_op jit(solution)/shard_map/scatter | solution.py:95
  155.7 6.0 convert_element_type.100
  161.7 0.0 reduce-scatter.9.cloned.1.call-update
  161.7 0.0 copy-start.7
  161.7 4.4 convolution_convert_fusion
  166.2 78.7 %fusion = bf16[16,2048]{1,0:T(8,128)(2,1)S(1)} fusion(bf16[384,2048]{1,0:T(8,128)(2,1)S(1)} %convolution_convert_fusion), kind=kCustom, calls=%all-reduce-scatter | all-reduce-scatter fusion | flops 1048577 | bytes 1639424
  244.9 2.5 collective-permute-start.6
  247.4 1.9 collective-permute-start.5
  249.4 10.2 %collective-permute-start.7 = (bf16[12,2048]{1,0:T(8,128)(2,1)S(1)}, bf16[12,2048]{1,0:T(8,128)(2,1)S(1)}, u32[]{:S(2)}, u32[]{:S(2)}) collective-permute-start(bf16[12,2048]{1,0:T(8,128)(2,1)S(1)} %slice.6), channel_id=1, source_target_pairs={{0,64},{8,72},{16,80},{24,88},{32,96},{40,104},{48,112},{56,120},{... | collective-permute-start | bytes 147464
  259.5 1.9 collective-permute-start.4
  261.4 9.1 %collective-permute-start.3 = (bf16[16,2048]{1,0:T(8,128)(2,1)S(1)}, bf16[16,2048]{1,0:T(8,128)(2,1)S(1)}, u32[]{:S(2)}, u32[]{:S(2)}) collective-permute-start(bf16[16,2048]{1,0:T(8,128)(2,1)S(1)} %fusion), channel_id=1, source_target_pairs={{0,32},{8,40},{16,48},{24,56},{32,64},{40,72},{48,80},{56,88},{64,... | collective-permute-start | bytes 196616
  270.6 0.0 collective-permute-done.7
  270.6 1.9 collective-permute-start.2
  272.5 0.0 collective-permute-done.6
  272.5 4.0 collective-permute-start.1
  276.5 0.0 collective-permute-done.5
  276.5 3.4 collective-permute-start
  279.9 0.6 dynamic-slice.4
  281.2 0.0 collective-permute-done.4
  281.2 0.0 collective-permute-done.3
  281.2 2.2 collective-permute-done.1
  283.4 1.4 collective-permute-done
  284.8 1.4 concatenate.6
  286.3 0.7 copy.15
  287.0 36.3 %reduce-scatter.13.cloned.1.call-done = bf16[64,384]{1,0:T(8,128)(2,1)} async-done(((bf16[2048,384]{1,0:T(8,128)(2,1)}), bf16[64,384]{1,0:T(8,128)(2,1)}) %reduce-scatter.13.cloned.1.call-update) | async-done | bytes 49168 | tf_op jit(solution)/shard_map/reduce_scatter | solution.py:111
  323.3 1.4 bitcast_convert_fusion
  324.7 216.6 %reduce-scatter.11.cloned.1.call-done = bf16[64,384]{1,0:T(8,128)(2,1)} async-done(((bf16[2048,384]{1,0:T(8,128)(2,1)}), bf16[64,384]{1,0:T(8,128)(2,1)}) %reduce-scatter.11.cloned.1.call-update) | async-done | bytes 49168 | tf_op jit(solution)/shard_map/reduce_scatter | solution.py:108
  541.4 1.4 bitcast_convert_fusion.1
  542.8 41.2 %reduce-scatter.7.cloned.1.call-done = bf16[128,2048]{1,0:T(8,128)(2,1)} async-done(((bf16[1024,2048]{1,0:T(8,128)(2,1)}), bf16[128,2048]{1,0:T(8,128)(2,1)}) %reduce-scatter.7.cloned.1.call-update) | async-done | bytes 524304 | tf_op jit(solution)/shard_map/reduce_scatter | solution.py:98
  584.0 42.3 %reduce-scatter.9.cloned.1.call-done = bf16[128,2048]{1,0:T(8,128)(2,1)} async-done(((bf16[1024,2048]{1,0:T(8,128)(2,1)}), bf16[128,2048]{1,0:T(8,128)(2,1)}) %reduce-scatter.9.cloned.1.call-update) | async-done | bytes 524304 | tf_op jit(solution)/shard_map/reduce_scatter | solution.py:101
  (26 shorter events, 0.2 us)
Async XLA Ops:
  7.2 88.5 %copy-start = (bf16[1,384,2048]{2,1,0:T(8,128)(2,1)S(1)}, bf16[1,384,2048]{2,1,0:T(8,128)(2,1)}, u32[]{:S(2)}) copy-start(bf16[1,384,2048]{2,1,0:T(8,128)(2,1)} %param.12) | copy-start | bytes 4718596
  7.2 40.4 %all-gather.3.cloned.1.call-start = ((), (), s32[]{:S(2)}) async-start(), calls=%async_computation.4 | async-start | bytes 4718592 | tf_op jit(solution)/shard_map/all_gather | solution.py:65
  7.9 76.2 %all-gather.5.cloned.1.call-start = ((), (), s32[]{:S(2)}) async-start(), calls=%async_computation.6 | async-start | bytes 4718592 | tf_op jit(solution)/shard_map/all_gather | solution.py:66
  8.7 314.6 %reduce-scatter.13.cloned.1.call-start = ((), (), s32[]{:S(2)}) async-start(), calls=%async_computation.9 | async-start | bytes 1622016 | tf_op jit(solution)/shard_map/reduce_scatter | solution.py:111
  59.1 6.6 %copy-start.1 = (bf16[1024,2048]{1,0:T(8,128)(2,1)S(1)}, bf16[1024,2048]{1,0:T(8,128)(2,1)}, u32[]{:S(2)}) copy-start(bf16[1024,2048]{1,0:T(8,128)(2,1)} %gather_fusion.1) | copy-start | bytes 12582916
  59.1 6.6 %copy-start.3 = (bf16[1,2048,384]{2,1,0:T(8,128)(2,1)S(1)}, bf16[1,2048,384]{2,1,0:T(8,128)(2,1)}, u32[]{:S(2)}) copy-start(bf16[1,2048,384]{2,1,0:T(8,128)(2,1)} %param.10) | copy-start | bytes 4718596
  95.6 8.2 %copy-start.2 = (bf16[1024,2048]{1,0:T(8,128)(2,1)S(1)}, bf16[1024,2048]{1,0:T(8,128)(2,1)}, u32[]{:S(2)}) copy-start(bf16[1024,2048]{1,0:T(8,128)(2,1)} %gather_fusion.1) | copy-start | bytes 12582916
  103.0 0.9 copy-start.5
  107.7 433.7 %reduce-scatter.11.cloned.1.call-start = ((), (), s32[]{:S(2)}) async-start(), calls=%async_computation.8 | async-start | bytes 1622016 | tf_op jit(solution)/shard_map/reduce_scatter | solution.py:108
  114.0 470.0 %reduce-scatter.7.cloned.1.call-start = ((), (), s32[]{:S(2)}) async-start(), calls=%async_computation.5 | async-start | bytes 4718592 | tf_op jit(solution)/shard_map/reduce_scatter | solution.py:98
  136.4 489.9 %reduce-scatter.9.cloned.1.call-start = ((), (), s32[]{:S(2)}) async-start(), calls=%async_computation.7 | async-start | bytes 4718592 | tf_op jit(solution)/shard_map/reduce_scatter | solution.py:101
  136.7 3.7 copy-start.4
  136.7 3.7 copy-start.6
  161.7 118.2 %copy-start.7 = (u32[256]{0:T(256)S(1)}, u32[256]{0:T(256)}, u32[]{:S(2)}) copy-start(u32[256]{0:T(256)} %constant.53) | copy-start | bytes 3076
  244.9 27.6 %collective-permute-start.6 = (bf16[16,2048]{1,0:T(8,128)(2,1)S(1)}, bf16[16,2048]{1,0:T(8,128)(2,1)S(1)}, u32[]{:S(2)}, u32[]{:S(2)}) collective-permute-start(bf16[16,2048]{1,0:T(8,128)(2,1)S(1)} %fusion), channel_id=1, source_target_pairs={{0,56},{8,64},{16,72},{24,80},{32,88},{40,96},{48,104},{56,112},{6... | collective-permute-start | bytes 196616
  247.4 29.1 %collective-permute-start.5 = (bf16[16,2048]{1,0:T(8,128)(2,1)S(1)}, bf16[16,2048]{1,0:T(8,128)(2,1)S(1)}, u32[]{:S(2)}, u32[]{:S(2)}) collective-permute-start(bf16[16,2048]{1,0:T(8,128)(2,1)S(1)} %fusion), channel_id=1, source_target_pairs={{0,48},{8,56},{16,64},{24,72},{32,80},{40,88},{48,96},{56,104},{64... | collective-permute-start | bytes 196616
  249.4 21.2 %collective-permute-start.7 = (bf16[12,2048]{1,0:T(8,128)(2,1)S(1)}, bf16[12,2048]{1,0:T(8,128)(2,1)S(1)}, u32[]{:S(2)}, u32[]{:S(2)}) collective-permute-start(bf16[12,2048]{1,0:T(8,128)(2,1)S(1)} %slice.6), channel_id=1, source_target_pairs={{0,64},{8,72},{16,80},{24,88},{32,96},{40,104},{48,112},{56,120},{... | collective-permute-start | bytes 147464
  259.5 21.6 %collective-permute-start.4 = (bf16[16,2048]{1,0:T(8,128)(2,1)S(1)}, bf16[16,2048]{1,0:T(8,128)(2,1)S(1)}, u32[]{:S(2)}, u32[]{:S(2)}) collective-permute-start(bf16[16,2048]{1,0:T(8,128)(2,1)S(1)} %fusion), channel_id=1, source_target_pairs={{0,40},{8,48},{16,56},{24,64},{32,72},{40,80},{48,88},{56,96},{64,... | collective-permute-start | bytes 196616
  261.4 19.7 %collective-permute-start.3 = (bf16[16,2048]{1,0:T(8,128)(2,1)S(1)}, bf16[16,2048]{1,0:T(8,128)(2,1)S(1)}, u32[]{:S(2)}, u32[]{:S(2)}) collective-permute-start(bf16[16,2048]{1,0:T(8,128)(2,1)S(1)} %fusion), channel_id=1, source_target_pairs={{0,32},{8,40},{16,48},{24,56},{32,64},{40,72},{48,80},{56,88},{64,... | collective-permute-start | bytes 196616
  270.6 10.6 %collective-permute-start.2 = (bf16[16,2048]{1,0:T(8,128)(2,1)S(1)}, bf16[16,2048]{1,0:T(8,128)(2,1)S(1)}, u32[]{:S(2)}, u32[]{:S(2)}) collective-permute-start(bf16[16,2048]{1,0:T(8,128)(2,1)S(1)} %fusion), channel_id=1, source_target_pairs={{0,24},{8,32},{16,40},{24,48},{32,56},{40,64},{48,72},{56,80},{64,... | collective-permute-start | bytes 196616
  272.5 10.9 %collective-permute-start.1 = (bf16[16,2048]{1,0:T(8,128)(2,1)S(1)}, bf16[16,2048]{1,0:T(8,128)(2,1)S(1)}, u32[]{:S(2)}, u32[]{:S(2)}) collective-permute-start(bf16[16,2048]{1,0:T(8,128)(2,1)S(1)} %fusion), channel_id=1, source_target_pairs={{0,16},{8,24},{16,32},{24,40},{32,48},{40,56},{48,64},{56,72},{64,... | collective-permute-start | bytes 196616
  276.5 8.3 %collective-permute-start = (bf16[16,2048]{1,0:T(8,128)(2,1)S(1)}, bf16[16,2048]{1,0:T(8,128)(2,1)S(1)}, u32[]{:S(2)}, u32[]{:S(2)}) collective-permute-start(bf16[16,2048]{1,0:T(8,128)(2,1)S(1)} %fusion), channel_id=1, source_target_pairs={{0,8},{8,16},{16,24},{24,32},{32,40},{40,48},{48,56},{56,64},{64,7... | collective-permute-start | bytes 196616
Sparse Core Ops, SparseCore 0:
  9.9 37.6 all-gather.2
  49.4 34.6 all-gather.4
  107.8 215.4 reduce-scatter.12
  327.0 214.3 reduce-scatter.10
  544.4 39.5 reduce-scatter.6
  587.0 39.3 reduce-scatter.8
where the time goes:
time: 634 us; the launch traced here: 633 us
  waiting for transfers between devices  363 us (57%)
  blocking collectives  101 us (16%)
  matrix products  45.2 us (7%)
  other arithmetic  37.8 us (6%)
  local copies, waits for them, and re-layouts  35.9 us (6%)
  starting transfers between devices  35.5 us (6%)
  between operations  15.1 us (2%)
    reduce_scatter x1, waiting for transfers between devices, per_device(): lax.psum_scatter(acc_gate.astype(jnp.bfloat16), 'dp', scatter_dimension=0...  217 us
    unnamed x1, blocking collectives  78.7 us
    reduce_scatter x1, waiting for transfers between devices, per_device(): lax.psum_scatter(part_grad.astype(jnp.bfloat16), 'expert', scatter_dimens...  42.3 us
    reduce_scatter x1, waiting for transfers between devices, per_device(): lax.psum_scatter(part_out.astype(jnp.bfloat16), 'expert', scatter_dimensi...  41.2 us
    reduce_scatter x1, waiting for transfers between devices, per_device(): lax.psum_scatter(acc_up.astype(jnp.bfloat16), 'dp', scatter_dimension=0,...  36.3 us
    unnamed x8, starting transfers between devices  34.9 us
    all_gather x1, waiting for transfers between devices, per_device(): lax.all_gather(cotangent, 'expert', axis=0, tiled=True)  14.8 us
  transfers between devices with their start and end apart: 14, of which 8 were waited for; matrix products, arithmetic and copies ran while one was open for 27% of the time, Pallas kernels for 0%

commit v1 on v0

--- a/solution.py
+++ b/solution.py
@@ -2,6 +2,14 @@
 import jax.numpy as jnp
 from jax import lax
 from jax.sharding import PartitionSpec as P
+
+
+def gather_by_exchange(array, axis, dim):
+    peers = lax.axis_size(axis)
+    repeats = [peers if d == dim else 1 for d in range(array.ndim)]
+    return lax.all_to_all(
+        jnp.tile(array, repeats), axis, split_axis=dim, concat_axis=dim, tiled=True
+    )
 
 
 def expert_rows(inputs, out_grads, gate_col, gate_panel, up_panel, down_panel):
@@ -63,7 +71,7 @@
     down_panel = w_down[0]
     all_rows, all_cot, all_gates = (
         lax.all_gather(tokens, "expert", axis=0, tiled=True),
-        lax.all_gather(cotangent, "expert", axis=0, tiled=True),
+        gather_by_exchange(cotangent, "expert", 0),
         lax.all_gather(gates, "expert", axis=0, tiled=True),
     )
     all_ids = lax.all_gather(expert_ids, "expert", axis=0, tiled=True)

time: 634 us -> 673 us (1.062)
  blocking collectives: 101 us -> 163 us
  waiting for transfers between devices: 363 us -> 339 us
    all_gather x1, blocking collectives: 12.2 us -> 71 us  [per_device(): all_ids = lax.all_gather(expert_ids, 'expert', axis=0, tiled=True)]
    all_gather x1 -> x0, waiting for transfers between devices: 14.8 us -> none  [per_device(): lax.all_gather(cotangent, 'expert', axis=0, tiled=True)]
  transfers between devices with their start and end apart: 14 -> 14, of which waited for: 8 -> 6; matrix products, arithmetic and copies ran while one was open for 27% -> 25% of each run, Pallas kernels for 0% -> 0%
where the time goes in v1:
time: 673 us; the launch traced here: 672 us
  waiting for transfers between devices  339 us (50%)
  blocking collectives  163 us (24%)
  local copies, waits for them, and re-layouts  39.4 us (6%)
  matrix products  39.3 us (6%)
  starting transfers between devices  39 us (6%)
  other arithmetic  37.8 us (6%)
  between operations  14.8 us (2%)
    reduce_scatter x1, waiting for transfers between devices, per_device(): lax.psum_scatter(acc_gate.astype(jnp.bfloat16), 'dp', scatter_dimension=0...  217 us
    unnamed x1, blocking collectives  82 us
    all_gather x1, blocking collectives, per_device(): all_ids = lax.all_gather(expert_ids, 'expert', axis=0, tiled=True)  71 us
    reduce_scatter x1, waiting for transfers between devices, per_device(): lax.psum_scatter(part_grad.astype(jnp.bfloat16), 'expert', scatter_dimens...  42.3 us
    reduce_scatter x1, waiting for transfers between devices, per_device(): lax.psum_scatter(part_out.astype(jnp.bfloat16), 'expert', scatter_dimensi...  41.1 us
    reduce_scatter x1, waiting for transfers between devices, per_device(): lax.psum_scatter(acc_up.astype(jnp.bfloat16), 'dp', scatter_dimension=0,...  34.8 us
    unnamed x8, starting transfers between devices  33.7 us
  transfers between devices with their start and end apart: 14, of which 6 were waited for; matrix products, arithmetic and copies ran while one was open for 25% of the time, Pallas kernels for 0%

profile of v1, /device:TPU:2, one launch (start us, length us, event | category | flops | bytes accessed | tf_op | source)
XLA Modules:
  0.0 672.5 jit_solution(13478985650277986934)
XLA Ops:
  7.2 0.0 copy-start
  7.2 0.0 all-gather.2.cloned.1.call-start
  7.2 0.7 all-gather.2.cloned.1.call-update
  7.9 3.5 tile.2
  11.4 4.7 all-to-all-start
  16.1 0.0 reduce-scatter.13.cloned.1.call-start
  16.2 71.0 %all_gather.9 = s32[1024,4]{0,1:T(4,128)S(1)} all-gather(s32[128,4]{0,1:T(4,128)S(1)} %copy-done.7), channel_id=1, replica_groups=mesh['dp'=32,'expert'=8] {'expert'}, dimensions={0}, use_global_device_ids=true | all-gather | bytes 18432 | tf_op jit(solution)/shard_map/all_gather | solution.py:77
  87.2 0.3 reduce_window_sum.11
  87.5 9.9 %all_gather.10 = bf16[1024,4]{0,1:T(4,128)(2,1)S(1)} all-gather(bf16[128,4]{0,1:T(4,128)(2,1)S(1)} %copy-done.8), channel_id=1, replica_groups=mesh['dp'=32,'expert'=8] {'expert'}, dimensions={0}, use_global_device_ids=true | all-gather | bytes 9216 | tf_op jit(solution)/shard_map/all_gather | solution.py:75
  97.5 0.5 select_reduce_fusion
  98.0 0.1 broadcast_add_fusion
  98.1 9.1 %gather_fusion = bf16[1024]{0:T(1024)(128)(2,1)S(1)} fusion(bf16[1024,4]{0,1:T(4,128)(2,1)S(1)} %all_gather.10, s32[1024]{0:T(1024)S(1)} %bitcast.64), kind=kCustom, calls=%fused_computation | custom fusion | bytes 12288 | tf_op jit(solution)/shard_map/gather | solution.py:87
  107.2 0.0 all-to-all-done
  107.2 11.5 %gather_fusion.2 = bf16[1024,2048]{1,0:T(8,128)(2,1)} fusion(bf16[1024,2048]{1,0:T(8,128)(2,1)} %bitcast.11, s32[1024]{0:T(1024)S(1)} %broadcast_clamp_fusion), kind=kCustom, calls=%fused_computation.2 | custom fusion | bytes 8392704 | tf_op jit(solution)/shard_map/gather | solution.py:89
  118.7 11.5 %gather_fusion.1 = bf16[1024,2048]{1,0:T(8,128)(2,1)} fusion(bf16[1024,2048]{1,0:T(8,128)(2,1)} %all-gather.2.cloned.1.call-done, s32[1024]{0:T(1024)S(1)} %broadcast_clamp_fusion), kind=kCustom, calls=%fused_computation.1 | custom fusion | bytes 8392704 | tf_op jit(solution)/shard_map/gather | solution.py:86
  130.3 5.2 fusion.9
  135.5 2.4 fusion.11
  137.9 4.1 multiply_convert_fusion.4
  142.0 0.9 copy-done.5
  142.9 3.8 convolution_convert_fusion.1
  146.6 0.0 reduce-scatter.13.cloned.1.call-update
  146.7 0.2 reduce-scatter.11.cloned.1.call-start
  146.9 6.1 convolution_convert_fusion.2
  153.0 0.0 reduce-scatter.11.cloned.1.call-update
  153.0 0.0 reduce-scatter.7.cloned.1.call-start
  153.1 5.4 multiply_convert_fusion.1
  158.5 10.9 %scatter_custom_fusion = f32[1024,2048]{1,0:T(8,128)} fusion(s32[1024]{0:T(1024)S(1)} %bitcast.71, bf16[1024,2048]{1,0:T(8,128)(2,1)} %multiply_convert_fusion.1, f32[]{:T(128)} %constant.10.clone.1), kind=kCustom, calls=%fused_computation.9 | custom fusion | flops 2097152 | bytes 12582916 | tf_op jit(solution)/shard_map/scatter | solution.py:98
  169.4 6.0 convert_element_type.93
  175.4 0.0 reduce-scatter.7.cloned.1.call-update
  175.4 0.3 reduce-scatter.9.cloned.1.call-start
  175.7 0.0 copy-start.4
  175.7 3.7 fusion.22
  179.4 4.3 add_convert_fusion
  183.7 10.9 %scatter_custom_fusion.1 = f32[1024,2048]{1,0:T(8,128)} fusion(s32[1024]{0:T(1024)S(1)} %bitcast.72, bf16[1024,2048]{1,0:T(8,128)(2,1)} %add_convert_fusion, f32[]{:T(128)} %constant.10.clone.1), kind=kCustom, calls=%fused_computation.5 | custom fusion | flops 2097152 | bytes 12582916 | tf_op jit(solution)/shard_map/scatter | solution.py:103
  194.7 6.0 convert_element_type.100
  200.7 0.0 reduce-scatter.9.cloned.1.call-update
  200.7 0.0 copy-start.9
  200.7 4.4 convolution_convert_fusion
  205.2 82.0 %fusion = bf16[16,2048]{1,0:T(8,128)(2,1)S(1)} fusion(bf16[384,2048]{1,0:T(8,128)(2,1)S(1)} %convolution_convert_fusion), kind=kCustom, calls=%all-reduce-scatter | all-reduce-scatter fusion | flops 1048577 | bytes 1639424
  287.2 1.9 collective-permute-start.6
  289.1 1.9 collective-permute-start.5
  291.1 9.5 %collective-permute-start.7 = (bf16[12,2048]{1,0:T(8,128)(2,1)S(1)}, bf16[12,2048]{1,0:T(8,128)(2,1)S(1)}, u32[]{:S(2)}, u32[]{:S(2)}) collective-permute-start(bf16[12,2048]{1,0:T(8,128)(2,1)S(1)} %slice.6), channel_id=1, source_target_pairs={{0,64},{8,72},{16,80},{24,88},{32,96},{40,104},{48,112},{56,120},{... | collective-permute-start | bytes 147464
  300.6 1.9 collective-permute-start.4
  302.5 9.1 %collective-permute-start.3 = (bf16[16,2048]{1,0:T(8,128)(2,1)S(1)}, bf16[16,2048]{1,0:T(8,128)(2,1)S(1)}, u32[]{:S(2)}, u32[]{:S(2)}) collective-permute-start(bf16[16,2048]{1,0:T(8,128)(2,1)S(1)} %fusion), channel_id=1, source_target_pairs={{0,32},{8,40},{16,48},{24,56},{32,64},{40,72},{48,80},{56,88},{64,... | collective-permute-start | bytes 196616
  311.7 0.0 collective-permute-done.7
  311.7 1.9 collective-permute-start.2
  313.6 0.0 collective-permute-done.6
  313.6 4.0 collective-permute-start.1
  317.6 0.0 collective-permute-done.5
  317.6 3.4 collective-permute-start
  321.0 0.6 dynamic-slice.4
  322.3 0.0 collective-permute-done.4
  322.3 0.0 collective-permute-done.3
  322.3 0.0 collective-permute-done.2
  322.3 2.2 collective-permute-done.1
  324.5 1.4 collective-permute-done
  325.9 1.4 concatenate.6
  327.4 0.7 copy.15
  328.1 34.8 %reduce-scatter.13.cloned.1.call-done = bf16[64,384]{1,0:T(8,128)(2,1)} async-done(((bf16[2048,384]{1,0:T(8,128)(2,1)}), bf16[64,384]{1,0:T(8,128)(2,1)}) %reduce-scatter.13.cloned.1.call-update) | async-done | bytes 49168 | tf_op jit(solution)/shard_map/reduce_scatter | solution.py:119
  362.9 1.4 bitcast_convert_fusion
  364.4 216.8 %reduce-scatter.11.cloned.1.call-done = bf16[64,384]{1,0:T(8,128)(2,1)} async-done(((bf16[2048,384]{1,0:T(8,128)(2,1)}), bf16[64,384]{1,0:T(8,128)(2,1)}) %reduce-scatter.11.cloned.1.call-update) | async-done | bytes 49168 | tf_op jit(solution)/shard_map/reduce_scatter | solution.py:116
  581.2 1.4 bitcast_convert_fusion.1
  582.6 41.1 %reduce-scatter.7.cloned.1.call-done = bf16[128,2048]{1,0:T(8,128)(2,1)} async-done(((bf16[1024,2048]{1,0:T(8,128)(2,1)}), bf16[128,2048]{1,0:T(8,128)(2,1)}) %reduce-scatter.7.cloned.1.call-update) | async-done | bytes 524304 | tf_op jit(solution)/shard_map/reduce_scatter | solution.py:106
  623.7 42.3 %reduce-scatter.9.cloned.1.call-done = bf16[128,2048]{1,0:T(8,128)(2,1)} async-done(((bf16[1024,2048]{1,0:T(8,128)(2,1)}), bf16[128,2048]{1,0:T(8,128)(2,1)}) %reduce-scatter.9.cloned.1.call-update) | async-done | bytes 524304 | tf_op jit(solution)/shard_map/reduce_scatter | solution.py:109
  (30 shorter events, 0.2 us)
Async XLA Ops:
  7.2 130.7 %copy-start = (bf16[1,384,2048]{2,1,0:T(8,128)(2,1)S(1)}, bf16[1,384,2048]{2,1,0:T(8,128)(2,1)}, u32[]{:S(2)}) copy-start(bf16[1,384,2048]{2,1,0:T(8,128)(2,1)} %param.12) | copy-start | bytes 4718596
  7.2 111.5 %all-gather.2.cloned.1.call-start = ((), (), s32[]{:S(2)}) async-start(), calls=%async_computation.5 | async-start | bytes 4718592 | tf_op jit(solution)/shard_map/all_gather | solution.py:73
  11.4 4.7 copy-start.7
  11.4 76.1 %copy-start.8 = (bf16[128,4]{0,1:T(4,128)(2,1)S(1)}, bf16[128,4]{0,1:T(4,128)(2,1)}, u32[]{:S(2)}) copy-start(bf16[128,4]{0,1:T(4,128)(2,1)} %param.9) | copy-start | bytes 3076
  11.4 95.7 %all-to-all-start = ((bf16[8,128,2048]{2,1,0:T(8,128)(2,1)}), bf16[8,128,2048]{2,1,0:T(8,128)(2,1)}, u32[]{:S(2)}, u32[]{:S(2)}) async-start(bf16[8,128,2048]{2,1,0:T(8,128)(2,1)} %tile.2), calls=%async_computation.1 | async-start | bytes 8388608 | tf_op jit(solution)/shard_map/all_to_all | solution.py:10
  16.1 346.8 %reduce-scatter.13.cloned.1.call-start = ((), (), s32[]{:S(2)}) async-start(), calls=%async_computation.9 | async-start | bytes 1622016 | tf_op jit(solution)/shard_map/reduce_scatter | solution.py:119
  130.2 5.2 copy-start.2
  130.2 5.2 copy-start.3
  135.5 2.4 copy-start.1
  142.0 0.9 copy-start.5
  146.7 434.5 %reduce-scatter.11.cloned.1.call-start = ((), (), s32[]{:S(2)}) async-start(), calls=%async_computation.8 | async-start | bytes 1622016 | tf_op jit(solution)/shard_map/reduce_scatter | solution.py:116
  153.0 470.7 %reduce-scatter.7.cloned.1.call-start = ((), (), s32[]{:S(2)}) async-start(), calls=%async_computation.6 | async-start | bytes 4718592 | tf_op jit(solution)/shard_map/reduce_scatter | solution.py:106
  175.4 490.5 %reduce-scatter.9.cloned.1.call-start = ((), (), s32[]{:S(2)}) async-start(), calls=%async_computation.7 | async-start | bytes 4718592 | tf_op jit(solution)/shard_map/reduce_scatter | solution.py:109
  175.7 3.7 copy-start.4
  175.7 3.7 copy-start.6
  200.7 120.3 %copy-start.9 = (u32[256]{0:T(256)S(1)}, u32[256]{0:T(256)}, u32[]{:S(2)}) copy-start(u32[256]{0:T(256)} %constant.53) | copy-start | bytes 3076
  287.2 26.4 %collective-permute-start.6 = (bf16[16,2048]{1,0:T(8,128)(2,1)S(1)}, bf16[16,2048]{1,0:T(8,128)(2,1)S(1)}, u32[]{:S(2)}, u32[]{:S(2)}) collective-permute-start(bf16[16,2048]{1,0:T(8,128)(2,1)S(1)} %fusion), channel_id=1, source_target_pairs={{0,56},{8,64},{16,72},{24,80},{32,88},{40,96},{48,104},{56,112},{6... | collective-permute-start | bytes 196616
  289.1 28.5 %collective-permute-start.5 = (bf16[16,2048]{1,0:T(8,128)(2,1)S(1)}, bf16[16,2048]{1,0:T(8,128)(2,1)S(1)}, u32[]{:S(2)}, u32[]{:S(2)}) collective-permute-start(bf16[16,2048]{1,0:T(8,128)(2,1)S(1)} %fusion), channel_id=1, source_target_pairs={{0,48},{8,56},{16,64},{24,72},{32,80},{40,88},{48,96},{56,104},{64... | collective-permute-start | bytes 196616
  291.1 20.6 %collective-permute-start.7 = (bf16[12,2048]{1,0:T(8,128)(2,1)S(1)}, bf16[12,2048]{1,0:T(8,128)(2,1)S(1)}, u32[]{:S(2)}, u32[]{:S(2)}) collective-permute-start(bf16[12,2048]{1,0:T(8,128)(2,1)S(1)} %slice.6), channel_id=1, source_target_pairs={{0,64},{8,72},{16,80},{24,88},{32,96},{40,104},{48,112},{56,120},{... | collective-permute-start | bytes 147464
  300.6 21.7 %collective-permute-start.4 = (bf16[16,2048]{1,0:T(8,128)(2,1)S(1)}, bf16[16,2048]{1,0:T(8,128)(2,1)S(1)}, u32[]{:S(2)}, u32[]{:S(2)}) collective-permute-start(bf16[16,2048]{1,0:T(8,128)(2,1)S(1)} %fusion), channel_id=1, source_target_pairs={{0,40},{8,48},{16,56},{24,64},{32,72},{40,80},{48,88},{56,96},{64,... | collective-permute-start | bytes 196616
  302.5 19.7 %collective-permute-start.3 = (bf16[16,2048]{1,0:T(8,128)(2,1)S(1)}, bf16[16,2048]{1,0:T(8,128)(2,1)S(1)}, u32[]{:S(2)}, u32[]{:S(2)}) collective-permute-start(bf16[16,2048]{1,0:T(8,128)(2,1)S(1)} %fusion), channel_id=1, source_target_pairs={{0,32},{8,40},{16,48},{24,56},{32,64},{40,72},{48,80},{56,88},{64,... | collective-permute-start | bytes 196616
  311.7 10.6 %collective-permute-start.2 = (bf16[16,2048]{1,0:T(8,128)(2,1)S(1)}, bf16[16,2048]{1,0:T(8,128)(2,1)S(1)}, u32[]{:S(2)}, u32[]{:S(2)}) collective-permute-start(bf16[16,2048]{1,0:T(8,128)(2,1)S(1)} %fusion), channel_id=1, source_target_pairs={{0,24},{8,32},{16,40},{24,48},{32,56},{40,64},{48,72},{56,80},{64,... | collective-permute-start | bytes 196616
  313.6 10.9 %collective-permute-start.1 = (bf16[16,2048]{1,0:T(8,128)(2,1)S(1)}, bf16[16,2048]{1,0:T(8,128)(2,1)S(1)}, u32[]{:S(2)}, u32[]{:S(2)}) collective-permute-start(bf16[16,2048]{1,0:T(8,128)(2,1)S(1)} %fusion), channel_id=1, source_target_pairs={{0,16},{8,24},{16,32},{24,40},{32,48},{40,56},{48,64},{56,72},{64,... | collective-permute-start | bytes 196616
  317.6 8.3 %collective-permute-start = (bf16[16,2048]{1,0:T(8,128)(2,1)S(1)}, bf16[16,2048]{1,0:T(8,128)(2,1)S(1)}, u32[]{:S(2)}, u32[]{:S(2)}) collective-permute-start(bf16[16,2048]{1,0:T(8,128)(2,1)S(1)} %fusion), channel_id=1, source_target_pairs={{0,8},{8,16},{16,24},{24,32},{32,40},{40,48},{48,56},{56,64},{64,7... | collective-permute-start | bytes 196616
Sparse Core Ops, SparseCore 0:
  9.9 59.3 all-gather.1
  146.8 216.0 reduce-scatter.12
  366.8 214.3 reduce-scatter.10
  584.1 39.4 reduce-scatter.6
  626.6 39.2 reduce-scatter.8
